TPU v7x, 256 devices: a whole 4x4x8 slice. The times are simulated.
256 devices in a mesh: prompt: 8 (over x, y_lo), tensor: 32 (over z, y_hi, core).
Axes of the slice: x: 4, y: 4 (y_hi: 2, y_lo: 2; y = y_hi * 2 + y_lo), z: 8, core: 2. Of those that a mesh axis runs over, the one named last changes fastest.
Arguments:
- tokens: bfloat16 [8, 128, 8192], P('prompt')
- gate_weight: bfloat16 [8192, 28672], P('prompt', 'tensor'), may hold values from -0.0625 to 0.0625
- up_weight: bfloat16 [8192, 28672], P('prompt', 'tensor'), may hold values from -0.0625 to 0.0625
- down_weight: bfloat16 [28672, 8192], P('tensor', 'prompt')
- norm_gain: float32 [8192], P('prompt'), may hold values from 0.1 to 1.9
- unembed: bfloat16 [8192, 86016], P('prompt', 'tensor'), may hold values from -0.5 to 0.5
- guidance: float32 [8], replicated, may hold values from -1.5 to 2.5
- logit_bias: float32 [128, 86016], P('prompt', 'tensor'), may hold values from -2 to 322
Outputs:
- log_probs: float32 [128, 86016], P('prompt', 'tensor')
All inputs are finite; a program needn't handle non-finite values.
Results may differ from a plain program's by a relative error of at most 0.0025.
Values may be sent and summed in bfloat16 or wider, within the bound.
No kernel may reach another device: no remote copies, remote signals or barrier semaphores. Data moves between devices by JAX's collectives and lax.ppermute only.
A program may use at most 64 MiB of HBM per device.

v0:
```python
import jax
import jax.numpy as jnp
from jax import lax
from jax.sharding import Mesh
from jax.sharding import PartitionSpec as P

D = 8192
PROMPT = ("prompt_0", "prompt_1")


def own_rows(so_far, axes):
    for axis in axes:
        so_far = lax.psum_scatter(so_far, axis, scatter_dimension=0, tiled=True)
    return so_far


def copy_for_each(array, axis):
    peers = lax.axis_size(axis)
    return lax.all_to_all(
        jnp.broadcast_to(array[None], (peers, *array.shape)), axis, 0, 0, tiled=True
    )


def joined_along(tiles, dim):
    tiles = jnp.moveaxis(tiles, 0, dim)
    shape = tiles.shape
    return tiles.reshape(*shape[:dim], shape[dim] * shape[dim + 1], *shape[dim + 2 :])


def collect(array, axis, dim):
    tiles = copy_for_each(array, axis)
    return joined_along(tiles, dim)


def of_everyone(array, axis):
    return copy_for_each(array, axis).sum(axis=0)


def cut_along(array, dim, peers):
    shape = array.shape
    tiles = array.reshape(*shape[:dim], peers, shape[dim] // peers, *shape[dim + 1 :])
    return jnp.moveaxis(tiles, dim, 0)


def sent_and_summed(array, axis, dim):
    tiles = cut_along(array, dim, lax.axis_size(axis))
    arrived = lax.all_to_all(tiles, axis, split_axis=0, concat_axis=0, tiled=True)
    return arrived.sum(axis=0)


def gathered_once(array, axis):
    leaves = jax.tree.leaves(array)
    turns = sorted(range(len(leaves)), key=lambda k: -leaves[k].size)
    width = (1, *leaves[turns[0]].shape)[-1]
    lines = [
        jnp.pad(leaves[k].reshape(-1), (0, -leaves[k].size % width)).reshape(-1, width)
        for k in turns
    ]
    both, at, found = (copy_for_each(jnp.concatenate(lines), axis), 0, {})
    for k, line in zip(turns, lines):
        slab = both[:, at : at + len(line)].reshape(len(both), -1)
        found[k] = slab[:, : leaves[k].size].reshape(-1, *leaves[k].shape)
        at += len(line)
    numbers = iter(range(len(leaves)))
    return jax.tree.map(lambda _: found[next(numbers)], array)


def combined_pairwise(pieces, combine):
    while len(jax.tree.leaves(pieces)[0]) > 1:
        pieces = jax.vmap(combine)(
            *(jax.tree.map(lambda part: part[side::2], pieces) for side in (0, 1))
        )
    return jax.tree.map(lambda part: part[0], pieces)


def merged(array, axis, combine):
    pieces = gathered_once(array, axis)
    return combined_pairwise(pieces, combine)


def combine_lse(first, second):
    top = jnp.maximum(first[0], second[0])
    total = first[1] * jnp.exp(first[0] - top) + second[1] * jnp.exp(second[0] - top)
    return (top, total)


def local(tokens, gate_weight, up_weight, down_weight, norm_gain, unembed, guidance, logit_bias):
    variants = lax.axis_size(PROMPT)
    rows = tokens.shape[1]
    share = gate_weight.shape[0]
    spread = lax.all_to_all(tokens, PROMPT, split_axis=2, concat_axis=0, tiled=True)
    flat = spread.reshape(variants * rows, share)
    gate_part = jnp.dot(flat, gate_weight, preferred_element_type=jnp.float32)
    up_part = jnp.dot(flat, up_weight, preferred_element_type=jnp.float32)
    gate_up = own_rows(jnp.concatenate([gate_part, up_part], axis=1), PROMPT)
    width = gate_weight.shape[1]
    hidden = (jax.nn.silu(gate_up[:, :width]) * gate_up[:, width:]).astype(jnp.bfloat16)
    partial_branch = jnp.dot(
        collect(hidden, PROMPT, 0), down_weight, preferred_element_type=jnp.float32
    )
    mine = lax.psum_scatter(partial_branch, "tensor", scatter_dimension=0, tiled=True)
    count = mine.shape[0]
    start = lax.axis_index("tensor") * count
    state = lax.dynamic_slice_in_dim(flat, start, count, 0).astype(jnp.float32) + mine
    square = of_everyone(jnp.sum(state * state, axis=1), PROMPT)
    owned = (state * lax.rsqrt(square / D + 1e-05)[:, None] * norm_gain).astype(jnp.bfloat16)
    normed = lax.all_gather(owned, "tensor", axis=0, tiled=True)
    blocks = normed.reshape(variants, rows, share)
    mixed = jnp.tensordot(guidance, blocks.astype(jnp.float32), axes=1)
    high = mixed.astype(jnp.bfloat16)
    low = (mixed - high.astype(jnp.float32)).astype(jnp.bfloat16)
    stacked = jnp.concatenate([high, low], axis=0)
    product = jnp.dot(stacked, unembed, preferred_element_type=jnp.float32)
    scores = (
        sent_and_summed(
            product[: rows // variants * lax.axis_size(PROMPT)]
            + product[rows // variants * lax.axis_size(PROMPT) :],
            PROMPT,
            0,
        )
        + logit_bias
    )
    local_top = jnp.max(scores, axis=1)
    local_total = jnp.sum(jnp.exp(scores - local_top[:, None]), axis=1)
    top, total_exp = merged((local_top, local_total), "tensor", combine_lse)
    return scores - top[:, None] - jnp.log(total_exp)[:, None]


def solution(mesh):
    finer = Mesh(
        mesh.devices.reshape(4, 2, mesh.shape["tensor"]), ("prompt_0", "prompt_1", "tensor")
    )
    placed = (
        P(PROMPT, None, None),
        P(PROMPT, "tensor"),
        P(PROMPT, "tensor"),
        P("tensor", PROMPT),
        P(PROMPT),
        P(PROMPT, "tensor"),
        P(),
        P(PROMPT, "tensor"),
    )
    return jax.shard_map(
        local, mesh=finer, in_specs=placed, out_specs=P(PROMPT, "tensor"), check_vma=False
    )
```

profile of v0, /device:TPU:1, one launch (start us, length us, event | category | flops | bytes accessed | tf_op | source)
XLA Modules:
  0.0 547.3 jit_solution(13178497889290529071)
XLA Ops:
  6.5 9.6 %copy.23 = bf16[1,128,8192]{1,0,2:T(2,128)(2,1)} copy(bf16[1,128,8192]{2,1,0:T(8,128)(2,1)} %param.8) | data formatting | bytes 4194304 | tf_op args[0]
  16.2 0.5 broadcast.18
  16.7 46.5 %reduce.1 = bf16[8192,128]{1,0:T(8,128)(2,1)} reduce(bf16[8192,1,128]{2,1,0:T(2,128)(2,1)} %bitcast.47, bf16[]{:T(256)} %broadcast.18), dimensions={1}, to_apply=%bitcast.29.reduce_sub_computation | reduce | bytes 4194306
  63.2 5.8 %reshape.57 = bf16[8,2,65536]{2,1,0:T(2,128)(2,1)} reshape(bf16[8192,128]{1,0:T(8,128)(2,1)} %reduce.1) | data formatting | bytes 4194304
  69.0 31.1 %all_to_all.36 = bf16[8,2,65536]{2,1,0:T(2,128)(2,1)} all-to-all(bf16[8,2,65536]{2,1,0:T(2,128)(2,1)} %reshape.57), channel_id=1, replica_groups=mesh['prompt_0'=4,'prompt_1'=2,'tensor'=32] {'prompt_0','prompt_1'}, dimensions={0} | all-to-all | bytes 4194304 | tf_op jit(solution)/shard_map/all_to_all | solution.py:91
  100.1 6.8 %reshape.58 = bf16[8192,1,128]{2,1,0:T(2,128)(2,1)} reshape(bf16[8,2,65536]{2,1,0:T(2,128)(2,1)} %all_to_all.36) | data formatting | bytes 4194304
  106.8 3.8 copy.30
  110.6 4.0 copy.24
  114.6 4.5 fusion.15
  119.1 2.2 fusion.16
  121.3 3.7 pad_maximum_fusion
  125.0 78.3 %reduce-scatter.4.cloned.1.call-done = f32[256,1792]{0,1:T(8,128)} async-done(((f32[1024,1792]{0,1:T(8,128)}), f32[256,1792]{0,1:T(8,128)}) %reduce-scatter.4.cloned.1.call-update) | async-done | bytes 1835024 | tf_op jit(solution)/shard_map/reduce_scatter | solution.py:13
  203.4 0.2 reduce-scatter.8.cloned.1.call-start
  203.6 36.1 %reduce-scatter.6.cloned.1.call-done = f32[128,1792]{0,1:T(8,128)} async-done(((f32[256,1792]{0,1:T(8,128)}), f32[128,1792]{0,1:T(8,128)}) %reduce-scatter.6.cloned.1.call-update) | async-done | bytes 917520 | tf_op jit(solution)/shard_map/reduce_scatter | solution.py:13
  239.7 1.3 fusion.7
  240.9 0.2 copy.25
  241.1 0.2 broadcast_in_dim.6
  241.4 26.5 %all_to_all.37 = bf16[8,128,896]{2,1,0:T(8,128)(2,1)S(1)} all-to-all(bf16[8,128,896]{2,1,0:T(8,128)(2,1)S(1)} %broadcast_in_dim.6), channel_id=1, replica_groups=mesh['prompt_0'=4,'prompt_1'=2,'tensor'=32] {'prompt_0','prompt_1'}, dimensions={0} | all-to-all | bytes 3670016 | tf_op jit(solution)/shard_map/all_to_all | solution.py:19
  267.9 4.3 fusion.17
  272.3 124.4 %reduce-scatter.8.cloned.1.call-done = f32[32,1024]{1,0:T(8,128)} async-done(((f32[1024,1024]{1,0:T(8,128)}), f32[32,1024]{1,0:T(8,128)}) %reduce-scatter.8.cloned.1.call-update) | async-done | bytes 131088 | tf_op jit(solution)/shard_map/reduce_scatter | solution.py:101
  396.6 1.0 multiply_reduce_fusion
  397.7 9.7 %all_to_all.38 = f32[8,1,32]{2,1,0:T(1,128)S(1)} all-to-all(f32[8,1,32]{2,1,0:T(1,128)S(1)} %broadcast_in_dim.7), channel_id=1, replica_groups=mesh['prompt_0'=4,'prompt_1'=2,'tensor'=32] {'prompt_0','prompt_1'}, dimensions={0} | all-to-all | bytes 2048 | tf_op jit(solution)/shard_map/all_to_all | solution.py:19
  407.4 1.6 multiply_convert_fusion
  409.0 83.2 %all-gather.2.cloned.1.call-done = bf16[1024,1024]{1,0:T(8,128)(2,1)} async-done(((bf16[32,1024]{1,0:T(8,128)(2,1)}), bf16[1024,1024]{1,0:T(8,128)(2,1)}) %all-gather.2.cloned.1.call-update) | async-done | bytes 2097168 | tf_op jit(solution)/shard_map/all_gather | solution.py:107
  492.3 3.0 fusion
  495.5 4.2 fusion.2
  499.7 0.1 slice_add_fusion
  499.9 22.2 %all_to_all.39 = f32[8,16,2688]{2,1,0:T(8,128)S(1)} all-to-all(f32[8,16,2688]{2,1,0:T(8,128)S(1)} %bitcast.50), channel_id=1, replica_groups=mesh['prompt_0'=4,'prompt_1'=2,'tensor'=32] {'prompt_0','prompt_1'}, dimensions={0} | all-to-all | bytes 2752512 | tf_op jit(solution)/shard_map/all_to_all | solution.py:47
  522.1 0.1 fusion.11
  522.3 0.2 exponential_reduce_fusion
  522.5 17.0 %all_to_all.40 = f32[32,2,16]{2,1,0:T(2,128)S(1)} all-to-all(f32[32,2,16]{2,1,0:T(2,128)S(1)} %broadcast_in_dim.8), channel_id=1, replica_groups=mesh['prompt_0'=4,'prompt_1'=2,'tensor'=32] {'tensor'}, dimensions={0} | all-to-all | bytes 8192 | tf_op jit(solution)/shard_map/all_to_all | solution.py:19
  540.0 0.8 subtract_subtract_fusion
  (49 shorter events, 0.9 us)
Async XLA Ops:
  6.5 261.4 %copy-start = (bf16[896,1024]{1,0:T(8,128)(2,1)S(1)}, bf16[896,1024]{1,0:T(8,128)(2,1)}, u32[]{:S(2)}) copy-start(bf16[896,1024]{1,0:T(8,128)(2,1)} %param.11) | copy-start | bytes 5505028
  6.5 196.8 %reduce-scatter.4.cloned.1.call-start = ((), (), s32[]{:S(2)}) async-start(), calls=%async_computation.8 | async-start | bytes 9175040 | tf_op jit(solution)/shard_map/reduce_scatter | solution.py:13
  114.6 4.5 copy-start.1
  114.6 4.5 copy-start.5
  125.0 114.7 %reduce-scatter.6.cloned.1.call-start = ((), (), s32[]{:S(2)}) async-start(), calls=%async_computation.9 | async-start | bytes 2752512 | tf_op jit(solution)/shard_map/reduce_scatter | solution.py:13
  203.4 193.3 %reduce-scatter.8.cloned.1.call-start = ((), (), s32[]{:S(2)}) async-start(), calls=%async_computation.10 | async-start | bytes 4325376 | tf_op jit(solution)/shard_map/reduce_scatter | solution.py:101
  272.2 135.2 %copy-start.3 = (f32[1024]{0:T(1024)S(1)}, f32[1024]{0:T(1024)}, u32[]{:S(2)}) copy-start(f32[1024]{0:T(1024)} %param.12) | copy-start | bytes 12292
  272.2 220.1 %copy-start.4 = (f32[8]{0:T(128)S(1)}, f32[8]{0:T(128)}, u32[]{:S(2)}) copy-start(f32[8]{0:T(128)} %param.14) | copy-start | bytes 100
  272.2 220.1 %all-gather.2.cloned.1.call-start = ((), (), s32[]{:S(2)}) async-start(), calls=%async_computation.11 | async-start | bytes 2162688 | tf_op jit(solution)/shard_map/all_gather | solution.py:107
  499.8 22.3 %copy-start.2 = (f32[16,2688]{1,0:T(8,128)S(1)}, f32[16,2688]{1,0:T(8,128)}, u32[]{:S(2)}) copy-start(f32[16,2688]{1,0:T(8,128)} %param.15) | copy-start | bytes 516100
Sparse Core Ops, SparseCore 0:
  125.1 78.1 reduce-scatter.3
  205.8 33.7 reduce-scatter.5
  272.3 124.2 reduce-scatter.7
  409.1 83.0 all-gather.1
where the time goes:
time: 548 us; the launch traced here: 547 us
  waiting for transfers between devices  322 us (59%)
  blocking collectives  106 us (19%)
  other arithmetic  55.7 us (10%)
  local copies, waits for them, and re-layouts  31.3 us (6%)
  matrix products  18.1 us (3%)
  between operations  13.3 us (2%)
    reduce_scatter x1, waiting for transfers between devices, local(): lax.psum_scatter(partial_branch, 'tensor', scatter_dimension=0, tiled=True)  124 us
    reduce_scatter x2, waiting for transfers between devices, own_rows(): so_far = lax.psum_scatter(so_far, axis, scatter_dimension=0, tiled=True)  114 us
    all_gather x1, waiting for transfers between devices, local(): normed = lax.all_gather(owned, 'tensor', axis=0, tiled=True)  83.2 us
    all_to_all x3, blocking collectives, copy_for_each(): lax.all_to_all(jnp.broadcast_to(array[None], (peers, *array.shape)), axis...  53.2 us
    unnamed x1, other arithmetic  46.5 us
    all_to_all x1, blocking collectives, local(): lax.all_to_all(tokens, PROMPT, split_axis=2, concat_axis=0, tiled=True)  31.1 us
    unnamed x17, local copies, waits for them, and re-layouts  26.5 us
    all_to_all x1, blocking collectives, sent_and_summed(): lax.all_to_all(tiles, axis, split_axis=0, concat_axis=0, tiled=True)  22.2 us
  transfers between devices with their start and end apart: 4, of which 4 were waited for; matrix products, arithmetic and copies ran while one was open for 0% of the time, Pallas kernels for 0%

commit v1 on v0

--- a/solution.py
+++ b/solution.py
@@ -1,3 +1,4 @@
+import functools
 import jax
 import jax.numpy as jnp
 from jax import lax
@@ -6,6 +7,17 @@
 
 D = 8192
 PROMPT = ("prompt_0", "prompt_1")
+
+
+def sides_answer(unit, axis_tag, axis_no, join_dim):
+    carry_out = jax.lax.axis_size(axis_tag)
+    met_up = jnp.split(unit, carry_out, axis=axis_no)
+    current_value = jnp.stack(met_up)
+    base_arr = jax.lax.all_to_all(current_value, axis_tag, 0, 0)
+    return jnp.concatenate(base_arr, axis=join_dim)
+
+
+spot_render = functools.partial(sides_answer, axis_tag=PROMPT, axis_no=2, join_dim=0)
 
 
 def own_rows(so_far, axes):
@@ -88,7 +100,7 @@
     variants = lax.axis_size(PROMPT)
     rows = tokens.shape[1]
     share = gate_weight.shape[0]
-    spread = lax.all_to_all(tokens, PROMPT, split_axis=2, concat_axis=0, tiled=True)
+    spread = spot_render(tokens)
     flat = spread.reshape(variants * rows, share)
     gate_part = jnp.dot(flat, gate_weight, preferred_element_type=jnp.float32)
     up_part = jnp.dot(flat, up_weight, preferred_element_type=jnp.float32)

time: 548 us -> 477 us (0.87)
  other arithmetic: 55.7 us -> 9.15 us
  local copies, waits for them, and re-layouts: 31.3 us -> 8.81 us
    unnamed x1 -> x0, other arithmetic: 46.5 us -> none
    unnamed x17 -> x21, local copies, waits for them, and re-layouts: 26.5 us -> 7.01 us
where the time goes in v1:
time: 477 us; the launch traced here: 476 us
  waiting for transfers between devices  322 us (68%)
  blocking collectives  106 us (22%)
  matrix products  15.9 us (3%)
  between operations  13.3 us (3%)
  other arithmetic  9.15 us (2%)
  local copies, waits for them, and re-layouts  8.81 us (2%)
    reduce_scatter x1, waiting for transfers between devices, local(): lax.psum_scatter(partial_branch, 'tensor', scatter_dimension=0, tiled=True)  125 us
    reduce_scatter x2, waiting for transfers between devices, own_rows(): so_far = lax.psum_scatter(so_far, axis, scatter_dimension=0, tiled=True)  114 us
    all_gather x1, waiting for transfers between devices, local(): normed = lax.all_gather(owned, 'tensor', axis=0, tiled=True)  83.6 us
    all_to_all x3, blocking collectives, copy_for_each(): lax.all_to_all(jnp.broadcast_to(array[None], (peers, *array.shape)), axis...  52.6 us
    all_to_all x1, blocking collectives, sides_answer(): base_arr = jax.lax.all_to_all(current_value, axis_tag, 0, 0)  31.6 us
    all_to_all x1, blocking collectives, sent_and_summed(): lax.all_to_all(tiles, axis, split_axis=0, concat_axis=0, tiled=True)  22.2 us
  transfers between devices with their start and end apart: 4, of which 4 were waited for; matrix products, arithmetic and copies ran while one was open for 0% of the time, Pallas kernels for 0%

profile of v1, /device:TPU:1, one launch (start us, length us, event | category | flops | bytes accessed | tf_op | source)
XLA Modules:
  0.0 475.9 jit_solution(11970162396997846273)
XLA Ops:
  6.5 1.1 bitcast_dynamic-update-slice_fusion.7
  7.6 1.0 bitcast_dynamic-update-slice_fusion.6
  8.6 1.0 bitcast_dynamic-update-slice_fusion.5
  9.6 1.0 bitcast_dynamic-update-slice_fusion.4
  10.6 1.0 bitcast_dynamic-update-slice_fusion.3
  11.5 1.0 bitcast_dynamic-update-slice_fusion.2
  12.5 1.0 bitcast_dynamic-update-slice_fusion.1
  13.5 1.0 bitcast_dynamic-update-slice_fusion
  14.5 31.6 %all_to_all.26 = bf16[8,1,128,1024]{3,2,1,0:T(8,128)(2,1)S(1)} all-to-all(bf16[8,1,128,1024]{3,2,1,0:T(8,128)(2,1)S(1)} %bitcast_dynamic-update-slice_fusion), channel_id=1, replica_groups=mesh['prompt_0'=4,'prompt_1'=2,'tensor'=32] {'prompt_0','prompt_1'}, dimensions={0} | all-to-all | bytes 4194304 | tf_op jit(solution)/shard_map/all_to_all | solution.py:16
  46.0 2.2 fusion.15
  48.3 2.2 fusion.16
  50.5 3.7 pad_maximum_fusion
  54.2 77.6 %reduce-scatter.4.cloned.1.call-done = f32[256,1792]{0,1:T(8,128)} async-done(((f32[1024,1792]{0,1:T(8,128)}), f32[256,1792]{0,1:T(8,128)}) %reduce-scatter.4.cloned.1.call-update) | async-done | bytes 1835024 | tf_op jit(solution)/shard_map/reduce_scatter | solution.py:25
  131.9 36.3 %reduce-scatter.6.cloned.1.call-done = f32[128,1792]{0,1:T(8,128)} async-done(((f32[256,1792]{0,1:T(8,128)}), f32[128,1792]{0,1:T(8,128)}) %reduce-scatter.6.cloned.1.call-update) | async-done | bytes 917520 | tf_op jit(solution)/shard_map/reduce_scatter | solution.py:25
  168.2 1.3 fusion.7
  169.5 0.2 copy.14
  169.6 0.2 broadcast_in_dim.6
  169.9 26.3 %all_to_all.27 = bf16[8,128,896]{2,1,0:T(8,128)(2,1)S(1)} all-to-all(bf16[8,128,896]{2,1,0:T(8,128)(2,1)S(1)} %broadcast_in_dim.6), channel_id=1, replica_groups=mesh['prompt_0'=4,'prompt_1'=2,'tensor'=32] {'prompt_0','prompt_1'}, dimensions={0} | all-to-all | bytes 3670016 | tf_op jit(solution)/shard_map/all_to_all | solution.py:31
  196.2 4.3 fusion.17
  200.5 124.7 %reduce-scatter.8.cloned.1.call-done = f32[32,1024]{1,0:T(8,128)} async-done(((f32[1024,1024]{1,0:T(8,128)}), f32[32,1024]{1,0:T(8,128)}) %reduce-scatter.8.cloned.1.call-update) | async-done | bytes 131088 | tf_op jit(solution)/shard_map/reduce_scatter | solution.py:113
  325.2 1.0 multiply_reduce_fusion
  326.3 9.3 %all_to_all.28 = f32[8,1,32]{2,1,0:T(1,128)S(1)} all-to-all(f32[8,1,32]{2,1,0:T(1,128)S(1)} %broadcast_in_dim.7), channel_id=1, replica_groups=mesh['prompt_0'=4,'prompt_1'=2,'tensor'=32] {'prompt_0','prompt_1'}, dimensions={0} | all-to-all | bytes 2048 | tf_op jit(solution)/shard_map/all_to_all | solution.py:31
  335.6 1.6 multiply_convert_fusion
  337.2 83.6 %all-gather.2.cloned.1.call-done = bf16[1024,1024]{1,0:T(8,128)(2,1)} async-done(((bf16[32,1024]{1,0:T(8,128)(2,1)}), bf16[1024,1024]{1,0:T(8,128)(2,1)}) %all-gather.2.cloned.1.call-update) | async-done | bytes 2097168 | tf_op jit(solution)/shard_map/all_gather | solution.py:119
  420.9 3.0 fusion
  424.1 4.2 fusion.2
  428.3 0.1 slice_add_fusion
  428.5 22.2 %all_to_all.29 = f32[8,16,2688]{2,1,0:T(8,128)S(1)} all-to-all(f32[8,16,2688]{2,1,0:T(8,128)S(1)} %bitcast.58), channel_id=1, replica_groups=mesh['prompt_0'=4,'prompt_1'=2,'tensor'=32] {'prompt_0','prompt_1'}, dimensions={0} | all-to-all | bytes 2752512 | tf_op jit(solution)/shard_map/all_to_all | solution.py:59
  450.8 0.1 fusion.11
  450.9 0.2 exponential_reduce_fusion
  451.1 17.0 %all_to_all.30 = f32[32,2,16]{2,1,0:T(2,128)S(1)} all-to-all(f32[32,2,16]{2,1,0:T(2,128)S(1)} %broadcast_in_dim.8), channel_id=1, replica_groups=mesh['prompt_0'=4,'prompt_1'=2,'tensor'=32] {'tensor'}, dimensions={0} | all-to-all | bytes 8192 | tf_op jit(solution)/shard_map/all_to_all | solution.py:31
  468.6 0.8 subtract_subtract_fusion
  (52 shorter events, 1.0 us)
Async XLA Ops:
  6.5 189.6 %copy-start = (bf16[896,1024]{1,0:T(8,128)(2,1)S(1)}, bf16[896,1024]{1,0:T(8,128)(2,1)}, u32[]{:S(2)}) copy-start(bf16[896,1024]{1,0:T(8,128)(2,1)} %param.11) | copy-start | bytes 5505028
  6.5 125.3 %reduce-scatter.4.cloned.1.call-start = ((), (), s32[]{:S(2)}) async-start(), calls=%async_computation.8 | async-start | bytes 9175040 | tf_op jit(solution)/shard_map/reduce_scatter | solution.py:25
  14.5 31.6 %copy-start.5 = (bf16[1024,896]{1,0:T(8,128)(2,1)S(1)}, bf16[1024,896]{1,0:T(8,128)(2,1)}, u32[]{:S(2)}) copy-start(bf16[1024,896]{1,0:T(8,128)(2,1)} %param.9) | copy-start | bytes 5505028
  46.0 2.2 copy-start.1
  46.0 2.3 copy-start.6
  54.2 114.0 %reduce-scatter.6.cloned.1.call-start = ((), (), s32[]{:S(2)}) async-start(), calls=%async_computation.9 | async-start | bytes 2752512 | tf_op jit(solution)/shard_map/reduce_scatter | solution.py:25
  131.9 193.3 %reduce-scatter.8.cloned.1.call-start = ((), (), s32[]{:S(2)}) async-start(), calls=%async_computation.10 | async-start | bytes 4325376 | tf_op jit(solution)/shard_map/reduce_scatter | solution.py:113
  200.4 135.1 %copy-start.3 = (f32[1024]{0:T(1024)S(1)}, f32[1024]{0:T(1024)}, u32[]{:S(2)}) copy-start(f32[1024]{0:T(1024)} %param.12) | copy-start | bytes 12292
  200.5 220.4 %copy-start.4 = (f32[8]{0:T(128)S(1)}, f32[8]{0:T(128)}, u32[]{:S(2)}) copy-start(f32[8]{0:T(128)} %param.14) | copy-start | bytes 100
  200.5 220.4 %all-gather.2.cloned.1.call-start = ((), (), s32[]{:S(2)}) async-start(), calls=%async_computation.11 | async-start | bytes 2162688 | tf_op jit(solution)/shard_map/all_gather | solution.py:119
  428.5 22.3 %copy-start.2 = (f32[16,2688]{1,0:T(8,128)S(1)}, f32[16,2688]{1,0:T(8,128)}, u32[]{:S(2)}) copy-start(f32[16,2688]{1,0:T(8,128)} %param.15) | copy-start | bytes 516100
Sparse Core Ops, SparseCore 0:
  54.3 77.4 reduce-scatter.3
  134.3 33.7 reduce-scatter.5
  200.6 124.5 reduce-scatter.7
  337.4 83.4 all-gather.1
